TPU v7x, 256 devices: a whole 4x4x8 slice. The times are simulated.
256 devices in a mesh: enc: 16 (over z, core), vocab: 8 (over x, y_hi), grp: 2 (over y_lo).
Axes of the slice: x: 4, y: 4 (y_hi: 2, y_lo: 2; y = y_hi * 2 + y_lo), z: 8, core: 2. Of those that a mesh axis runs over, the one named last changes fastest.
Arguments:
- hidden: bfloat16 [12288, 1024], P('enc', ('vocab', 'grp')), may hold values from -6 to 6
- dense_weight: bfloat16 [1024, 1024], P('enc'), may hold values from -0.1875 to 0.1875
- head_weight: bfloat16 [1024, 126976], P('enc', ('vocab', 'grp')), may hold values from -0.1875 to 0.1875
- head_bias: float32 [126976], P(('vocab', 'grp')), may hold values from -4 to 4
- lengths: int32 [48], P('enc'), may hold values from 64 to 256, as said below
- queries: bfloat16 [128, 126976], P('enc', ('vocab', 'grp')), may hold values from -0.25 to 0.25283518
- positives: int32 [128], replicated, may hold values from 0 to 47
Outputs:
- batch_loss: float32 [], replicated
- query_grad: float32 [128, 126976], P('enc', ('vocab', 'grp'))
- passage_grad: float32 [48, 126976], P('enc', ('vocab', 'grp'))
Inputs may be any that keep to these rules, and one draw needn't show every extreme that they name: `lengths`: each 3 passages in a row hold, among their first two, one with 256 valid tokens and one with 64.
All inputs are finite; a program needn't handle non-finite values.
Results may differ from a plain program's by a relative error of at most 0.035.
Values may be sent and summed in bfloat16 or wider, within the bound.
A program may use at most 128 MiB of HBM per device.

v0:
```python
import jax
import jax.numpy as jnp
from jax import lax
from jax.sharding import PartitionSpec as P


def finish_norm(pre_act):
    activated = jax.nn.gelu(pre_act, approximate=False)
    center = jnp.mean(activated, axis=-1, keepdims=True)
    spread = jnp.mean(jnp.square(activated - center), axis=-1, keepdims=True)
    return ((activated - center) * lax.rsqrt(spread + 1e-05)).astype(jnp.bfloat16)


def project(in_rows, dense_weight):
    pre_act = jnp.dot(
        in_rows,
        lax.all_gather(dense_weight, "enc", axis=0, tiled=True),
        preferred_element_type=jnp.float32,
    )
    return finish_norm(pre_act)


def pool_reps(logits, token_counts, seq_len):
    passages = token_counts.shape[0]
    by_passage = logits.reshape(passages, seq_len, logits.shape[1])
    positions = lax.broadcasted_iota(jnp.int32, (passages, seq_len), 1)
    is_valid = positions < token_counts[:, None]
    masked = jnp.where(is_valid[:, :, None], by_passage, -jnp.inf)
    peak_val = jnp.max(masked, axis=1)
    return jnp.log1p(jnp.maximum(peak_val, 0.0)).astype(jnp.bfloat16)


def softmax_grads(scores, chosen):
    peak_val = jnp.max(scores, axis=1, keepdims=True)
    log_total = jnp.log(jnp.sum(jnp.exp(scores - peak_val), axis=1, keepdims=True)) + peak_val
    columns = lax.broadcasted_iota(jnp.int32, scores.shape, 1)
    is_positive = columns == chosen[:, None]
    picked_score = jnp.sum(jnp.where(is_positive, scores, 0.0), axis=1)
    batch_loss = jnp.sum(log_total[:, 0] - picked_score)
    score_grad = (jnp.exp(scores - log_total) - is_positive.astype(jnp.float32)).astype(
        jnp.bfloat16
    )
    return (batch_loss, score_grad)


def per_device(hidden, dense_weight, head_weight, head_bias, lengths, queries, positives):
    pass_dev = lengths.shape[0]
    seq_len = hidden.shape[0] // pass_dev
    enc_index = lax.axis_index("enc")
    features_all = lax.all_gather(hidden, ("vocab", "grp"), axis=1, tiled=True)
    normed = project(features_all, dense_weight)
    logits = jnp.dot(
        normed,
        lax.all_gather(head_weight, "enc", axis=0, tiled=True),
        preferred_element_type=jnp.float32,
    )
    pass_reps = pool_reps(logits + head_bias, lengths, seq_len)
    all_queries = lax.all_gather(queries, "enc", axis=0, tiled=True)
    partial_value = lax.dot_general(
        all_queries, pass_reps, (((1,), (1,)), ((), ())), preferred_element_type=jnp.float32
    )
    local_scores = lax.psum(partial_value, ("vocab", "grp"))
    scores = lax.all_gather(local_scores, "enc", axis=1, tiled=True)
    loss_sum, score_grad = softmax_grads(scores, positives)
    batch_loss = loss_sum / scores.shape[0]
    own_grad = lax.dynamic_slice_in_dim(score_grad, enc_index * pass_dev, pass_dev, 1)
    query_grad = lax.psum_scatter(
        jnp.dot(own_grad, pass_reps, preferred_element_type=jnp.float32),
        "enc",
        scatter_dimension=0,
        tiled=True,
    )
    passage_grad = lax.dot_general(
        own_grad, all_queries, (((0,), (0,)), ((), ())), preferred_element_type=jnp.float32
    )
    return (batch_loss, query_grad, passage_grad)


def solution(mesh):
    placed = (
        P("enc", ("vocab", "grp")),
        P("enc", None),
        P("enc", ("vocab", "grp")),
        P(("vocab", "grp")),
        P("enc"),
        P("enc", ("vocab", "grp")),
        P(),
    )
    return jax.shard_map(
        per_device,
        mesh=mesh,
        in_specs=placed,
        out_specs=(P(), P("enc", ("vocab", "grp")), P("enc", ("vocab", "grp"))),
        check_vma=False,
    )
```

profile of v0, /device:TPU:2, one launch (start us, length us, event | category | flops | bytes accessed | tf_op | source)
XLA Modules:
  0.0 363.2 jit_solution(3995243074012879067)
XLA Ops:
  7.2 0.7 all-gather.6.cloned.1.call-update
  7.9 0.7 all-gather.8.cloned.1.call-update
  8.6 0.0 all-gather.10.cloned.1.call-start
  8.7 0.7 all-gather.10.cloned.1.call-update
  9.4 0.0 all-gather.12.cloned.1.call-start
  9.4 0.5 all-gather.12.cloned.1.call-update
  10.0 0.0 reduce-scatter.2.cloned.1.call-start
  10.0 0.7 iota_compare_fusion.1
  10.7 0.7 iota_compare_fusion
  11.4 50.6 %all-gather.6.cloned.1.call-done = bf16[768,1024]{0,1:T(8,128)(2,1)} async-done(((bf16[768,64]{0,1:T(8,128)(2,1)}), bf16[768,1024]{0,1:T(8,128)(2,1)}) %all-gather.6.cloned.1.call-update) | async-done | bytes 1572880 | tf_op jit(solution)/shard_map/all_gather | solution.py:50
  62.0 41.4 %all-gather.8.cloned.1.call-done = bf16[1024,1024]{1,0:T(8,128)(2,1)} async-done(((bf16[64,1024]{1,0:T(8,128)(2,1)}), bf16[1024,1024]{1,0:T(8,128)(2,1)}) %all-gather.8.cloned.1.call-update) | async-done | bytes 2097168 | tf_op jit(solution)/shard_map/all_gather | solution.py:17
  103.4 10.5 %fusion.17 = (f32[768]{0:T(1024)S(1)}, f32[768,1024]{1,0:T(8,128)S(1)}) fusion(bf16[768,1024]{0,1:T(8,128)(2,1)} %all-gather.6.cloned.1.call-done, bf16[1024,1024]{1,0:T(8,128)(2,1)} %all-gather.8.cloned.1.call-done), kind=kOutput, calls=%fused_computation.41 | convolution fusion | flops 1661730048 | bytes 6818816 | tf_op jit(solution)/shard_map/dot_general | solution.py:15
  114.0 0.4 multiply_reduce_fusion
  114.5 82.1 %all-gather.10.cloned.1.call-done = bf16[1024,7936]{1,0:T(8,128)(2,1)} async-done(((bf16[64,7936]{1,0:T(8,128)(2,1)}), bf16[1024,7936]{1,0:T(8,128)(2,1)}) %all-gather.10.cloned.1.call-update) | async-done | bytes 16252944 | tf_op jit(solution)/shard_map/all_gather | solution.py:54
  196.5 21.4 %convolution_add_fusion = f32[768,7936]{1,0:T(8,128)} fusion(bf16[1024,7936]{1,0:T(8,128)(2,1)} %all-gather.10.cloned.1.call-done, f32[7936]{0:T(1024)S(1)} %copy-done.2, f32[768,1024]{1,0:T(8,128)S(1)} %get-tuple-element.8, f32[768]{0:T(1024)S(1)} %add_rsqrt_fusion, f32[768]{0:T(1024)S(1)} %broadcast_multiply_fusion), kind=kOutput, calls=%fused_computation.1 | convolution fusion | flops 12490702848 | bytes 43815936 | tf_op jit(solution)/shard_map/dot_general | solution.py:52
  217.9 9.4 %select_reduce_fusion = f32[3,7936]{1,0:T(4,128)S(1)} fusion(f32[3,256,7936]{2,1,0:T(8,128)} %bitcast.14, pred[3,256]{1,0:T(4,128)(4,1)S(1)} %iota_compare_fusion.1), kind=kLoop, calls=%fused_computation | loop fusion | flops 12165888 | bytes 24475392 | tf_op jit(solution)/shard_map/reduce_max | solution.py:29
  227.4 9.2 %all-gather.12.cloned.1.call-done = bf16[128,7936]{1,0:T(8,128)(2,1)} async-done(((bf16[8,7936]{1,0:T(8,128)(2,1)}), bf16[128,7936]{1,0:T(8,128)(2,1)}) %all-gather.12.cloned.1.call-update) | async-done | bytes 2031632 | tf_op jit(solution)/shard_map/all_gather | solution.py:58
  236.5 2.2 convolution_bitcast_fusion
  238.7 34.3 %psum.7 = f32[128,3]{0,1:T(4,128)S(1)} all-reduce(f32[128,3]{0,1:T(4,128)S(1)} %convolution_bitcast_fusion), channel_id=1, replica_groups=mesh['enc'=16,'vocab'=8,'grp'=2] {'vocab','grp'}, use_global_device_ids=true, to_apply=%region_3.4 | all-reduce | flops 384 | bytes 3072 | tf_op jit(solution)/shard_map/psum | solution.py:62
  273.0 15.7 %all-gather = f32[16,3,128]{2,1,0:T(4,128)S(1)} all-gather(f32[1,3,128]{2,1,0:T(4,128)S(1)} %bitcast.17), channel_id=1, replica_groups=mesh['enc'=16,'vocab'=8,'grp'=2] {'enc'}, dimensions={0}, use_global_device_ids=true | all-gather | bytes 26112 | tf_op jit(solution)/shard_map/all_gather | solution.py:63
  288.8 0.6 subtract_reduce_fusion
  289.4 2.7 fusion.14
  292.7 1.0 fusion.20
  293.8 61.7 %reduce-scatter.2.cloned.1.call-done = f32[8,7936]{1,0:T(8,128)} async-done(((f32[128,7936]{1,0:T(8,128)}), f32[8,7936]{1,0:T(8,128)}) %reduce-scatter.2.cloned.1.call-update) | async-done | bytes 253968 | tf_op jit(solution)/shard_map/reduce_scatter | solution.py:67
  (14 shorter events, 0.2 us)
Async XLA Ops:
  7.2 54.9 %all-gather.6.cloned.1.call-start = ((), (), s32[]{:S(2)}) async-start(), calls=%async_computation.1 | async-start | bytes 1671168 | tf_op jit(solution)/shard_map/all_gather | solution.py:50
  7.9 95.5 %all-gather.8.cloned.1.call-start = ((), (), s32[]{:S(2)}) async-start(), calls=%async_computation.2 | async-start | bytes 2228224 | tf_op jit(solution)/shard_map/all_gather | solution.py:17
  8.6 187.9 %all-gather.10.cloned.1.call-start = ((), (), s32[]{:S(2)}) async-start(), calls=%async_computation.3 | async-start | bytes 17268736 | tf_op jit(solution)/shard_map/all_gather | solution.py:54
  9.4 227.2 %all-gather.12.cloned.1.call-start = ((), (), s32[]{:S(2)}) async-start(), calls=%async_computation.4 | async-start | bytes 2158592 | tf_op jit(solution)/shard_map/all_gather | solution.py:58
  10.0 345.5 %reduce-scatter.2.cloned.1.call-start = ((), (), s32[]{:S(2)}) async-start(), calls=%async_computation.5 | async-start | bytes 4317184 | tf_op jit(solution)/shard_map/reduce_scatter | solution.py:67
  114.0 82.6 %copy-start.2 = (f32[7936]{0:T(1024)S(1)}, f32[7936]{0:T(1024)}, u32[]{:S(2)}) copy-start(f32[7936]{0:T(1024)} %param.10) | copy-start | bytes 95236
  217.9 70.8 %copy-start.1 = (s32[128]{0:T(128)S(1)}, s32[128]{0:T(128)}, u32[]{:S(2)}) copy-start(s32[128]{0:T(128)} %param.13) | copy-start | bytes 1540
  289.4 3.3 copy-start
Sparse Core Ops, SparseCore 0:
  10.5 51.5 all-gather.5
  63.9 39.5 all-gather.7
  105.3 91.2 all-gather.9
  198.2 38.2 all-gather.11
  292.2 63.2 reduce-scatter.1
where the time goes:
time: 363 us
  waiting for transfers between devices  248 us (68%)
  blocking collectives  50 us (14%)
  matrix products  37.8 us (10%)
  between operations  15.6 us (4%)
  other arithmetic  12 us (3%)
    all_gather x1, waiting for transfers between devices, per_device(): lax.all_gather(head_weight, 'enc', axis=0, tiled=True)  82.1 us
    reduce_scatter x1, waiting for transfers between devices, per_device(): lax.psum_scatter(jnp.dot(own_grad, pass_reps, preferred_element_type=jnp....  61.7 us
    all_gather x1, waiting for transfers between devices, per_device(): features_all = lax.all_gather(hidden, ('vocab', 'grp'), axis=1, tiled=True)  50.6 us
    all_gather x1, waiting for transfers between devices, project(): lax.all_gather(dense_weight, 'enc', axis=0, tiled=True)  41.4 us
    psum x1, blocking collectives, per_device(): local_scores = lax.psum(partial_value, ('vocab', 'grp'))  34.3 us
    dot_general x1, matrix products, per_device(): jnp.dot(normed, lax.all_gather(head_weight, 'enc', axis=0, tiled=True), p...  21.4 us
    all_gather x1, blocking collectives, per_device(): scores = lax.all_gather(local_scores, 'enc', axis=1, tiled=True)  15.7 us
    dot_general x1, matrix products, project(): jnp.dot(in_rows, lax.all_gather(dense_weight, 'enc', axis=0, tiled=True),...  10.5 us
  transfers between devices with their start and end apart: 5, of which 5 were waited for; matrix products, arithmetic and copies ran while one was open for 12% of the time, Pallas kernels for 0%

commit v1 on v0

--- a/solution.py
+++ b/solution.py
@@ -59,7 +59,7 @@
     partial_value = lax.dot_general(
         all_queries, pass_reps, (((1,), (1,)), ((), ())), preferred_element_type=jnp.float32
     )
-    local_scores = lax.psum(partial_value, ("vocab", "grp"))
+    local_scores = jnp.sum(lax.all_gather(partial_value, ("vocab", "grp")), axis=0)
     scores = lax.all_gather(local_scores, "enc", axis=1, tiled=True)
     loss_sum, score_grad = softmax_grads(scores, positives)
     batch_loss = loss_sum / scores.shape[0]

time: 363 us -> 349 us (0.961)
  blocking collectives: 50 us -> 38.7 us
    psum x1 -> x0, blocking collectives: 34.3 us -> none  [per_device(): local_scores = lax.psum(partial_value, ('vocab', 'grp'))]
    all_gather x0 -> x1, blocking collectives: none -> 23 us  [per_device(): lax.all_gather(partial_value, ('vocab', 'grp'))]
  transfers between devices with their start and end apart: 5 -> 5, of which waited for: 5 -> 5; matrix products, arithmetic and copies ran while one was open for 12% -> 13% of each run, Pallas kernels for 0% -> 0%
where the time goes in v1:
time: 349 us
  waiting for transfers between devices  245 us (70%)
  blocking collectives  38.7 us (11%)
  matrix products  37.8 us (11%)
  between operations  15.6 us (4%)
  other arithmetic  12 us (3%)
    all_gather x1, waiting for transfers between devices, per_device(): lax.all_gather(head_weight, 'enc', axis=0, tiled=True)  82.1 us
    reduce_scatter x1, waiting for transfers between devices, per_device(): lax.psum_scatter(jnp.dot(own_grad, pass_reps, preferred_element_type=jnp....  59 us
    all_gather x1, waiting for transfers between devices, per_device(): features_all = lax.all_gather(hidden, ('vocab', 'grp'), axis=1, tiled=True)  50.6 us
    all_gather x1, waiting for transfers between devices, project(): lax.all_gather(dense_weight, 'enc', axis=0, tiled=True)  41.4 us
    all_gather x1, blocking collectives, per_device(): lax.all_gather(partial_value, ('vocab', 'grp'))  23 us
    dot_general x1, matrix products, per_device(): jnp.dot(normed, lax.all_gather(head_weight, 'enc', axis=0, tiled=True), p...  21.4 us
    all_gather x1, blocking collectives, per_device(): scores = lax.all_gather(local_scores, 'enc', axis=1, tiled=True)  15.7 us
    dot_general x1, matrix products, project(): jnp.dot(in_rows, lax.all_gather(dense_weight, 'enc', axis=0, tiled=True),...  10.5 us
  transfers between devices with their start and end apart: 5, of which 5 were waited for; matrix products, arithmetic and copies ran while one was open for 13% of the time, Pallas kernels for 0%

profile of v1, /device:TPU:2, one launch (start us, length us, event | category | flops | bytes accessed | tf_op | source)
XLA Modules:
  0.0 349.2 jit_solution(5108966183055949884)
XLA Ops:
  7.2 0.7 all-gather.7.cloned.1.call-update
  7.9 0.7 all-gather.9.cloned.1.call-update
  8.6 0.0 all-gather.11.cloned.1.call-start
  8.7 0.7 all-gather.11.cloned.1.call-update
  9.4 0.0 all-gather.13.cloned.1.call-start
  9.4 0.5 all-gather.13.cloned.1.call-update
  10.0 0.0 reduce-scatter.2.cloned.1.call-start
  10.0 0.7 iota_compare_fusion.1
  10.7 0.7 iota_compare_fusion
  11.4 50.6 %all-gather.7.cloned.1.call-done = bf16[768,1024]{0,1:T(8,128)(2,1)} async-done(((bf16[768,64]{0,1:T(8,128)(2,1)}), bf16[768,1024]{0,1:T(8,128)(2,1)}) %all-gather.7.cloned.1.call-update) | async-done | bytes 1572880 | tf_op jit(solution)/shard_map/all_gather | solution.py:50
  62.0 41.4 %all-gather.9.cloned.1.call-done = bf16[1024,1024]{1,0:T(8,128)(2,1)} async-done(((bf16[64,1024]{1,0:T(8,128)(2,1)}), bf16[1024,1024]{1,0:T(8,128)(2,1)}) %all-gather.9.cloned.1.call-update) | async-done | bytes 2097168 | tf_op jit(solution)/shard_map/all_gather | solution.py:17
  103.4 10.5 %fusion.17 = (f32[768]{0:T(1024)S(1)}, f32[768,1024]{1,0:T(8,128)S(1)}) fusion(bf16[768,1024]{0,1:T(8,128)(2,1)} %all-gather.7.cloned.1.call-done, bf16[1024,1024]{1,0:T(8,128)(2,1)} %all-gather.9.cloned.1.call-done), kind=kOutput, calls=%fused_computation.42 | convolution fusion | flops 1661730048 | bytes 6818816 | tf_op jit(solution)/shard_map/dot_general | solution.py:15
  114.0 0.4 multiply_reduce_fusion
  114.5 82.1 %all-gather.11.cloned.1.call-done = bf16[1024,7936]{1,0:T(8,128)(2,1)} async-done(((bf16[64,7936]{1,0:T(8,128)(2,1)}), bf16[1024,7936]{1,0:T(8,128)(2,1)}) %all-gather.11.cloned.1.call-update) | async-done | bytes 16252944 | tf_op jit(solution)/shard_map/all_gather | solution.py:54
  196.5 21.4 %convolution_add_fusion = f32[768,7936]{1,0:T(8,128)} fusion(bf16[1024,7936]{1,0:T(8,128)(2,1)} %all-gather.11.cloned.1.call-done, f32[7936]{0:T(1024)S(1)} %copy-done.2, f32[768,1024]{1,0:T(8,128)S(1)} %get-tuple-element.8, f32[768]{0:T(1024)S(1)} %add_rsqrt_fusion, f32[768]{0:T(1024)S(1)} %broadcast_multiply_fusion), kind=kOutput, calls=%fused_computation.1 | convolution fusion | flops 12490702848 | bytes 43815936 | tf_op jit(solution)/shard_map/dot_general | solution.py:52
  217.9 9.4 %select_reduce_fusion = f32[3,7936]{1,0:T(4,128)S(1)} fusion(f32[3,256,7936]{2,1,0:T(8,128)} %bitcast.19, pred[3,256]{1,0:T(4,128)(4,1)S(1)} %iota_compare_fusion.1), kind=kLoop, calls=%fused_computation | loop fusion | flops 12165888 | bytes 24475392 | tf_op jit(solution)/shard_map/reduce_max | solution.py:29
  227.4 9.2 %all-gather.13.cloned.1.call-done = bf16[128,7936]{1,0:T(8,128)(2,1)} async-done(((bf16[8,7936]{1,0:T(8,128)(2,1)}), bf16[128,7936]{1,0:T(8,128)(2,1)}) %all-gather.13.cloned.1.call-update) | async-done | bytes 2031632 | tf_op jit(solution)/shard_map/all_gather | solution.py:58
  236.5 2.2 convolution_bitcast_fusion
  238.7 23.0 %all-gather = f32[2048,3]{0,1:T(4,128)S(1)} all-gather(f32[128,3]{0,1:T(4,128)S(1)} %convolution_bitcast_fusion), channel_id=2, replica_groups=mesh['enc'=16,'vocab'=8,'grp'=2] {'vocab','grp'}, dimensions={0}, use_global_device_ids=true | all-gather | bytes 26112 | tf_op jit(solution)/shard_map/all_gather | solution.py:62
  261.8 15.7 %all-gather.1 = f32[16,3,128]{2,1,0:T(4,128)S(1)} all-gather(f32[1,3,128]{2,1,0:T(4,128)S(1)} %bitcast.23), channel_id=1, replica_groups=mesh['enc'=16,'vocab'=8,'grp'=2] {'enc'}, dimensions={0}, use_global_device_ids=true | all-gather | bytes 26112 | tf_op jit(solution)/shard_map/all_gather | solution.py:63
  277.5 0.6 subtract_reduce_fusion
  278.1 2.7 fusion.14
  281.5 1.0 fusion.20
  282.5 59.0 %reduce-scatter.2.cloned.1.call-done = f32[8,7936]{1,0:T(8,128)} async-done(((f32[128,7936]{1,0:T(8,128)}), f32[8,7936]{1,0:T(8,128)}) %reduce-scatter.2.cloned.1.call-update) | async-done | bytes 253968 | tf_op jit(solution)/shard_map/reduce_scatter | solution.py:67
  (15 shorter events, 0.2 us)
Async XLA Ops:
  7.2 54.9 %all-gather.7.cloned.1.call-start = ((), (), s32[]{:S(2)}) async-start(), calls=%async_computation.1 | async-start | bytes 1671168 | tf_op jit(solution)/shard_map/all_gather | solution.py:50
  7.9 95.5 %all-gather.9.cloned.1.call-start = ((), (), s32[]{:S(2)}) async-start(), calls=%async_computation.2 | async-start | bytes 2228224 | tf_op jit(solution)/shard_map/all_gather | solution.py:17
  8.6 187.9 %all-gather.11.cloned.1.call-start = ((), (), s32[]{:S(2)}) async-start(), calls=%async_computation.3 | async-start | bytes 17268736 | tf_op jit(solution)/shard_map/all_gather | solution.py:54
  9.4 227.2 %all-gather.13.cloned.1.call-start = ((), (), s32[]{:S(2)}) async-start(), calls=%async_computation.4 | async-start | bytes 2158592 | tf_op jit(solution)/shard_map/all_gather | solution.py:58
  10.0 331.6 %reduce-scatter.2.cloned.1.call-start = ((), (), s32[]{:S(2)}) async-start(), calls=%async_computation.5 | async-start | bytes 4317184 | tf_op jit(solution)/shard_map/reduce_scatter | solution.py:67
  114.0 82.6 %copy-start.2 = (f32[7936]{0:T(1024)S(1)}, f32[7936]{0:T(1024)}, u32[]{:S(2)}) copy-start(f32[7936]{0:T(1024)} %param.10) | copy-start | bytes 95236
  217.9 59.6 %copy-start.1 = (s32[128]{0:T(128)S(1)}, s32[128]{0:T(128)}, u32[]{:S(2)}) copy-start(s32[128]{0:T(128)} %param.13) | copy-start | bytes 1540
  278.1 3.3 copy-start
Sparse Core Ops, SparseCore 0:
  10.5 51.5 all-gather.6
  63.9 39.5 all-gather.8
  105.3 91.2 all-gather.10
  198.2 38.2 all-gather.12
  280.9 60.5 reduce-scatter.1
